TPU v7x, 32 devices: a whole 2x2x4 slice. The times are simulated.
32 devices in a mesh: dp: 2 (over x), ts: 16 (over z, y, core).
Axes of the slice: x: 2, y: 2, z: 4, core: 2. Of those that a mesh axis runs over, the one named last changes fastest.
Arguments:
- clip_video: bfloat16 [64, 4, 40, 128], P(('dp', 'ts')), may hold values from -6 to 6
- conv_weight: bfloat16 [3, 3, 3, 128, 128], replicated, may hold values from -0.109375 to 0.109375
- embed_weight: bfloat16 [128, 5120], replicated, may hold values from -0.5 to 0.5
- gain_spatial: float32 [5120], replicated, may hold values from 0.5 to 1.5
- gain_temporal: float32 [5120], replicated, may hold values from 0.5 to 1.5
- input_spatial: bfloat16 [5120, 384], P(('dp', 'ts')), may hold values from -0.078125 to 0.078125
- input_temporal: bfloat16 [5120, 384], P(('dp', 'ts')), may hold values from -0.078125 to 0.078125
- output_spatial: bfloat16 [128, 5120], replicated, may hold values from -2 to 2
- output_temporal: bfloat16 [128, 5120], replicated, may hold values from -2 to 2
- cotangent: bfloat16 [64, 4, 40, 5120], P(('dp', 'ts')), may hold values from -6 to 6
Outputs:
- layer_output: bfloat16 [64, 4, 40, 5120], P(('dp', 'ts'))
- grad_spatial: float32 [5120, 384], P(('dp', 'ts'))
All inputs are finite; a program needn't handle non-finite values.
Results may differ from a plain program's by a relative error of at most 0.015.
Values may be sent and summed in bfloat16 or wider, within the bound.
A program may use at most 128 MiB of HBM per device.

v0:
```python
import jax
import jax.numpy as jnp
from jax import lax
from jax.sharding import PartitionSpec as P

FR = 16
epsilon = 1e-06
masked = -1e30
F32 = jnp.float32
BF16 = jnp.bfloat16


def mm(a, b, dims=((1,), (0,))):
    return lax.dot_general(a, b, (dims, ((), ())), preferred_element_type=F32)


def mm_t(a, b):
    return mm(a, b, ((1,), (1,)))


def t_mm(a, b):
    return mm(a, b, ((0,), (0,)))


def wide_mm(a, b):
    high = b.astype(BF16)
    low = (b - high.astype(F32)).astype(BF16)
    return mm(a, high) + mm(a, low)


def conv_local(volume, weight, count):
    frames, height, columns, channels = volume.shape
    padded = jnp.pad(volume, ((0, 0), (1, 1), (1, 1), (0, 0)))
    summed = jnp.zeros((count * height * columns, weight.shape[-1]), F32)
    for a in range(3):
        for b in range(3):
            for e in range(3):
                window = padded[2 - a : 2 - a + count, b : b + height, e : e + columns, :]
                summed = summed + mm(window.reshape(-1, channels), weight[a, b, e])
    return summed


def attend_forward(q, k, v, allowed):
    scores = mm_t(q, k) * q.shape[-1] ** (-0.5)
    scores = jnp.where(allowed, scores, masked)
    raised = jnp.exp(scores - jnp.max(scores, axis=-1, keepdims=True))
    attend = raised / jnp.sum(raised, axis=-1, keepdims=True)
    return (mm(attend.astype(BF16), v).astype(BF16), attend)


def attend_backward(q, k, v, attend, g):
    scale = q.shape[-1] ** (-0.5)
    grad_attend = mm_t(g, v)
    grad_values = t_mm(attend.astype(BF16), g)
    inner = jnp.sum(grad_attend * attend, axis=-1, keepdims=True)
    grad_scores = (attend * (grad_attend - inner)).astype(BF16)
    grad_q = mm(grad_scores, k) * scale
    grad_k = t_mm(grad_scores, q) * scale
    return jnp.concatenate([grad_q, grad_k, grad_values], axis=-1).astype(BF16)


def shards(
    clip_video,
    conv_weight,
    embed_weight,
    gain_spatial,
    gain_temporal,
    input_spatial,
    input_temporal,
    output_spatial,
    output_temporal,
    cotangent,
):
    frames, height, columns, channels = clip_video.shape
    rows, triple = input_spatial.shape
    head = triple // 3
    width = embed_weight.shape[-1]
    places = height * columns
    tokens = frames * places
    ts = lax.axis_size("ts")
    team = FR // frames
    share = places // team
    groups = [[c * team + i for i in range(team)] for c in range(ts // team)]
    me = lax.axis_index("dp") * ts + lax.axis_index("ts")
    route = [(i - 1, i) for i in range(1, ts)]
    prior = lax.ppermute(clip_video, "ts", route)
    volume = jnp.concatenate([prior, clip_video], axis=0)
    basis = jnp.concatenate([embed_weight, output_spatial], axis=0)
    window = lax.dynamic_slice(basis, (0, me * rows), (basis.shape[0], rows)).astype(F32)
    gain_s = lax.dynamic_slice(gain_spatial, (me * rows,), (rows,))
    gain_t = lax.dynamic_slice(gain_temporal, (me * rows,), (rows,))
    embed_rows = (window[:channels] * gain_s).astype(BF16)
    part = jnp.concatenate(
        [mm(embed_rows, input_spatial), mm((window * gain_t).astype(BF16), input_temporal)], axis=0
    )
    mixed = lax.psum(part.astype(BF16), ("dp", "ts"))
    map_space, map_time = (mixed[:channels], mixed[channels:])
    gram = mm_t(basis, basis)
    cotangent_rows = cotangent.reshape(tokens, width)
    grad_mix_time = mm_t(cotangent_rows, output_temporal).astype(BF16)
    grad_direct = mm_t(cotangent_rows, output_spatial)
    features = jax.nn.gelu(conv_local(volume, conv_weight, frames), approximate=True).astype(BF16)
    squares = jnp.sum(
        wide_mm(features, gram[:channels, :channels]) * features.astype(F32), axis=-1, keepdims=True
    )
    factor_one = lax.rsqrt(jnp.maximum(squares, 0.0) / width + epsilon)
    packed_one = (mm(features, map_space) * factor_one).astype(BF16)
    place = jnp.arange(tokens)
    same_frame = place[:, None] // places == place[None, :] // places
    q, k, v = (packed_one[:, :head], packed_one[:, head : 2 * head], packed_one[:, 2 * head :])
    mixture_one, attend_one = attend_forward(q, k, v, same_frame)
    joint = jnp.concatenate([features, mixture_one], axis=-1)
    spread = wide_mm(joint, gram)
    squares = jnp.sum(spread * joint.astype(F32), axis=-1, keepdims=True)
    factor_two = lax.rsqrt(jnp.maximum(squares, 0.0) / width + epsilon)
    packed_two = (mm(joint, map_time) * factor_two).astype(BF16)
    sent = jnp.concatenate([packed_two, grad_mix_time], axis=-1).reshape(frames, places, 4 * head)
    got = lax.all_to_all(
        sent, "ts", split_axis=1, concat_axis=0, tiled=True, axis_index_groups=groups
    ).reshape(FR * share, 4 * head)
    spot = jnp.arange(FR * share)
    allowed = (spot[:, None] % share == spot[None, :] % share) & (spot[:, None] >= spot[None, :])
    tq, tk, tv, tg = (got[:, i * head : (i + 1) * head] for i in range(4))
    mixture_two, attend_two = attend_forward(tq, tk, tv, allowed)
    grad_two = attend_backward(tq, tk, tv, attend_two, tg)
    back = jnp.concatenate([mixture_two, grad_two], axis=-1).reshape(FR, share, 4 * head)
    home = lax.all_to_all(
        back, "ts", split_axis=0, concat_axis=1, tiled=True, axis_index_groups=groups
    ).reshape(tokens, 4 * head)
    mixture_two, grad_two = (home[:, :head], home[:, head:])
    output = mm(
        jnp.concatenate([joint, mixture_two], axis=-1),
        jnp.concatenate([basis, output_temporal], axis=0),
    ).astype(BF16)
    inner = jnp.sum(grad_two.astype(F32) * packed_two.astype(F32), axis=-1, keepdims=True)
    grad_mix_one = (
        grad_direct
        + factor_two * mm_t(grad_two, map_time[channels:])
        - factor_two**2 * inner / width * spread[:, channels:]
    ).astype(BF16)
    grad_one = attend_backward(q, k, v, attend_one, grad_mix_one)
    scaled = (features.astype(F32) * factor_one).astype(BF16)
    core = lax.psum(t_mm(scaled, grad_one).astype(BF16), ("dp", "ts"))
    return (output.reshape(frames, height, columns, width), t_mm(embed_rows, core))


def solution(mesh):
    placed = (
        P(("dp", "ts"), None, None, None),
        P(),
        P(),
        P(),
        P(),
        P(("dp", "ts"), None),
        P(("dp", "ts"), None),
        P(),
        P(),
        P(("dp", "ts"), None, None, None),
    )
    return jax.shard_map(
        shards,
        mesh=mesh,
        in_specs=placed,
        out_specs=(P(("dp", "ts"), None, None, None), P(("dp", "ts"), None)),
        check_vma=False,
    )
```

profile of v0, /device:TPU:8, one launch (start us, length us, event | category | flops | bytes accessed | tf_op | source)
XLA Modules:
  0.0 330.4 jit_solution(1640951019662262618)
XLA Ops:
  7.2 2.2 collective-permute-start
  9.4 2.5 constant_dynamic-update-slice_fusion.3
  11.9 2.5 constant_dynamic-update-slice_fusion.2
  14.4 1.0 dynamic-slice_convert_fusion
  15.4 0.8 dynamic_slice.10
  16.3 0.8 dynamic_slice.11
  17.0 1.2 convolution_convert_fusion.1
  18.2 1.1 convolution_convert_fusion.3
  19.3 0.7 pad_maximum_fusion.2
  20.1 3.5 %fusion.148 = f32[256,256]{1,0:T(8,128)S(1)} fusion(bf16[256,5120]{1,0:T(8,128)(2,1)} %constant_dynamic-update-slice_fusion.2), kind=kOutput, calls=%fused_computation.247 | convolution fusion | flops 671088640 | bytes 2883584 | tf_op jit(solution)/shard_map/dot_general | solution.py:14
  23.7 1.0 convolution_convert_fusion.4
  24.8 0.2 pad_slice_fusion
  25.1 0.8 copy-done.8
  26.2 0.2 convolution_add_fusion.27
  26.7 0.2 convolution_add_fusion.24
  27.1 0.2 convolution_add_fusion.21
  27.3 0.2 convolution_add_fusion.20
  27.5 0.2 convolution_add_fusion.19
  27.6 0.2 convolution_add_fusion.18
  27.9 0.2 convolution_add_fusion.16
  28.4 0.2 convolution_add_fusion.13
  28.6 0.2 convolution_add_fusion.12
  28.7 0.2 convolution_add_fusion.11
  28.9 0.2 convolution_add_fusion.10
  29.6 0.2 fusion.11
  30.0 0.2 fusion.43
  30.4 0.3 fusion.17
  30.7 120.0 %all-reduce.4.cloned.1.call-done = bf16[384,384]{1,0:T(8,128)(2,1)} async-done(((bf16[384,384]{1,0:T(8,128)(2,1)}), bf16[384,384]{1,0:T(8,128)(2,1)}) %all-reduce.4.cloned.1.call-update) | async-done | bytes 294928 | tf_op jit(solution)/shard_map/psum | solution.py:96
  150.8 1.1 fusion.7
  151.9 0.2 fusion.146
  152.3 0.7 copy-done.1
  153.0 0.3 convolution_convert_fusion.8
  153.3 0.2 fusion.71
  153.5 0.9 multiply_reduce_fusion.3
  154.4 0.3 fusion.8
  154.7 0.7 copy-done.7
  155.4 1.0 copy.12
  156.5 4.2 %all-to-all-start = ((bf16[2,160,512]{2,0,1:T(2,128)(2,1)}), bf16[2,160,512]{2,0,1:T(2,128)(2,1)}, u32[]{:S(2)}, u32[]{:S(2)}) async-start(bf16[2,160,512]{2,0,1:T(2,128)(2,1)} %copy.12), calls=%async_computation | async-start | bytes 655360 | tf_op jit(solution)/shard_map/all_to_all | solution.py:118
  160.7 6.2 %all-to-all-done = bf16[2,160,512]{2,0,1:T(2,128)(2,1)} async-done(((bf16[2,160,512]{2,0,1:T(2,128)(2,1)}), bf16[2,160,512]{2,0,1:T(2,128)(2,1)}, u32[]{:S(2)}, u32[]{:S(2)}) %all-to-all-start) | async-done | bytes 327712 | tf_op jit(solution)/shard_map/all_to_all | solution.py:118
  166.9 1.8 copy.13
  168.7 1.8 reshape.248
  170.5 1.2 fusion.147
  171.8 1.2 convolution_convert_fusion.7
  173.0 0.2 multiply_reduce_fusion.2
  173.4 0.3 fusion.12
  173.7 0.2 fusion.13
  173.9 0.2 convolution_convert_fusion.6
  174.1 0.8 pad_maximum_fusion.1
  174.9 1.8 reshape.249
  176.7 10.8 %all_to_all.30 = bf16[16,20,512]{2,1,0:T(8,128)(2,1)S(1)} all-to-all(bf16[16,20,512]{2,1,0:T(8,128)(2,1)} %reshape.249), channel_id=1, replica_groups={{0,1,2,3,4,5,6,7},{8,9,10,11,12,13,14,15},{16,17,18,19,20,21,22,23},{24..., dimensions={0} | all-to-all | bytes 655360 | tf_op jit(solution)/shard_map/all_to_all | solution.py:127
  187.5 0.3 copy.18
  187.8 0.9 copy.15
  188.7 1.8 reshape.250
  190.5 1.2 multiply_reduce_fusion.1
  191.7 1.3 convolution_multiply_fusion.6
  193.0 2.4 fusion.16
  195.5 0.3 multiply_reduce_fusion
  195.9 0.3 fusion.14
  196.2 0.2 fusion.15
  196.4 0.2 convolution_convert_fusion.5
  196.6 1.0 convolution_convert_fusion.2
  197.7 5.7 %convolution_convert_fusion = bf16[320,5120]{1,0:T(8,128)(2,1)} fusion(bf16[128,5120]{1,0:T(8,128)(2,1)} %param.18, bf16[128,5120]{1,0:T(8,128)(2,1)} %param.17, bf16[128,5120]{1,0:T(8,128)(2,1)} %param.12, bf16[320,128]{1,0:T(8,128)(2,1)S(1)} %slice-done, bf16[320,128]{1,0:T(8,128)(2,1)S(1)} %convolution_convert_fusion.8, bf16[320,128]{1,0:T(8,128)(2,1)S(1)} %fusion.43), kind=kOutput, calls=%fused_computation | convolution fusion | flops 1272463360 | bytes 7454720 | tf_op jit(solution)/shard_map/dot_general | solution.py:14
  203.3 118.4 %all-reduce.6.cloned.1.call-done = bf16[128,384]{1,0:T(8,128)(2,1)} async-done(((bf16[128,384]{1,0:T(8,128)(2,1)}), bf16[128,384]{1,0:T(8,128)(2,1)}) %all-reduce.6.cloned.1.call-update) | async-done | bytes 98320 | tf_op jit(solution)/shard_map/psum | solution.py:143
  321.7 1.9 fusion.129
  (62 shorter events, 3.2 us)
Async XLA Ops:
  7.2 16.5 %copy-start = (bf16[2,4,40,5120]{3,2,1,0:T(8,128)(2,1)S(1)}, bf16[2,4,40,5120]{3,2,1,0:T(8,128)(2,1)}, u32[]{:S(2)}) copy-start(bf16[2,4,40,5120]{3,2,1,0:T(8,128)(2,1)} %param.19) | copy-start | bytes 9830404
  7.2 143.6 %all-reduce.4.cloned.1.call-start = ((), (), s32[]{:S(2)}) async-start(), calls=%async_computation.2 | async-start | bytes 589824 | tf_op jit(solution)/shard_map/psum | solution.py:96
  7.2 17.5 %collective-permute-start = (bf16[2,4,40,128]{3,2,1,0:T(8,128)(2,1)}, bf16[2,4,40,128]{3,2,1,0:T(8,128)(2,1)S(1)}, u32[]{:S(2)}, u32[]{:S(2)}) collective-permute-start(bf16[2,4,40,128]{3,2,1,0:T(8,128)(2,1)} %param.10), channel_id=1, source_target_pairs={{0,1},{1,2},{2,3},{3,4},{4,5},{5,6},{6,7},{7,8},{8,9},{9,10},{10,1... | collective-permute-start | bytes 245768 | tf_op jit(solution)/shard_map/ppermute | solution.py:86
  9.4 7.6 %copy-start.13 = (bf16[160,384]{1,0:T(8,128)(2,1)S(1)}, bf16[160,384]{1,0:T(8,128)(2,1)}, u32[]{:S(2)}) copy-start(bf16[160,384]{1,0:T(8,128)(2,1)} %param.16) | copy-start | bytes 368644
  15.4 2.8 copy-start.6
  20.1 3.6 %copy-start.5 = (bf16[128,5120]{1,0:T(8,128)(2,1)S(1)}, bf16[128,5120]{1,0:T(8,128)(2,1)}, u32[]{:S(2)}) copy-start(bf16[128,5120]{1,0:T(8,128)(2,1)} %param.18) | copy-start | bytes 3932164
  23.6 6.8 %copy-start.3 = (f32[256,256]{1,0:T(8,128)}, f32[256,256]{1,0:T(8,128)S(1)}, u32[]{:S(2)}) copy-start(f32[256,256]{1,0:T(8,128)S(1)} %fusion.148) | copy-start | bytes 786436
  23.7 1.1 copy-start.12
  24.7 1.2 copy-start.8
  150.7 2.5 copy-start.4
  151.9 1.3 copy-start.10
  151.9 2.5 copy-start.14
  152.2 0.8 copy-start.1
  154.7 0.7 copy-start.7
  156.5 10.4 %all-to-all-start = ((bf16[2,160,512]{2,0,1:T(2,128)(2,1)}), bf16[2,160,512]{2,0,1:T(2,128)(2,1)}, u32[]{:S(2)}, u32[]{:S(2)}) async-start(bf16[2,160,512]{2,0,1:T(2,128)(2,1)} %copy.12), calls=%async_computation | async-start | bytes 655360 | tf_op jit(solution)/shard_map/all_to_all | solution.py:118
  160.7 161.0 %all-reduce.6.cloned.1.call-start = ((), (), s32[]{:S(2)}) async-start(), calls=%async_computation.3 | async-start | bytes 196608 | tf_op jit(solution)/shard_map/psum | solution.py:143
  170.5 2.5 copy-start.9
  193.0 2.4 copy-start.2
  193.0 2.4 copy-start.11
  195.7 1.9 slice-start
Sparse Core Ops, SparseCore 0:
  20.2 130.4 all-reduce.3
  197.8 123.8 all-reduce.5
where the time goes:
time: 331 us; the launch traced here: 330 us
  waiting for transfers between devices  245 us (74%)
  matrix products  31.3 us (9%)
  local copies, waits for them, and re-layouts  18.4 us (6%)
  between operations  14.5 us (4%)
  blocking collectives  10.8 us (3%)
  starting transfers between devices  6.42 us (2%)
  other arithmetic  4.29 us (1%)
    psum x1, waiting for transfers between devices, shards(): mixed = lax.psum(part.astype(BF16), ('dp', 'ts'))  120 us
    psum x1, waiting for transfers between devices, shards(): core = lax.psum(t_mm(scaled, grad_one).astype(BF16), ('dp', 'ts'))  118 us
    dot_general x54, matrix products, mm(): return lax.dot_general(a, b, (dims, ((), ())), preferred_element_type=F32)  31.3 us
    all_to_all x1, blocking collectives, shards(): lax.all_to_all(back, 'ts', split_axis=0, concat_axis=1, tiled=True, axis_...  10.8 us
  transfers between devices with their start and end apart: 4, of which 3 were waited for; matrix products, arithmetic and copies ran while one was open for 8% of the time, Pallas kernels for 0%

commit v1 on v0

--- a/solution.py
+++ b/solution.py
@@ -93,7 +93,7 @@
     part = jnp.concatenate(
         [mm(embed_rows, input_spatial), mm((window * gain_t).astype(BF16), input_temporal)], axis=0
     )
-    mixed = lax.psum(part.astype(BF16), ("dp", "ts"))
+    mixed = lax.psum(lax.psum(part.astype(BF16), "dp"), "ts")
     map_space, map_time = (mixed[:channels], mixed[channels:])
     gram = mm_t(basis, basis)
     cotangent_rows = cotangent.reshape(tokens, width)

time: 331 us -> 320 us (0.967)
  waiting for transfers between devices: 245 us -> 234 us
    psum x1 -> x2, waiting for transfers between devices: 120 us -> 109 us  [shards(): mixed = lax.psum(lax.psum(part.astype(BF16), 'dp'), 'ts')]
  transfers between devices with their start and end apart: 4 -> 5, of which waited for: 3 -> 4; matrix products, arithmetic and copies ran while one was open for 8% -> 8% of each run, Pallas kernels for 0% -> 0%
where the time goes in v1:
time: 320 us; the launch traced here: 319 us
  waiting for transfers between devices  234 us (73%)
  matrix products  31.3 us (10%)
  local copies, waits for them, and re-layouts  18.4 us (6%)
  between operations  14.2 us (4%)
  blocking collectives  10.8 us (3%)
  starting transfers between devices  6.81 us (2%)
  other arithmetic  4.3 us (1%)
    psum x1, waiting for transfers between devices, shards(): core = lax.psum(t_mm(scaled, grad_one).astype(BF16), ('dp', 'ts'))  118 us
    psum x2, waiting for transfers between devices, shards(): mixed = lax.psum(lax.psum(part.astype(BF16), 'dp'), 'ts')  109 us
    dot_general x54, matrix products, mm(): return lax.dot_general(a, b, (dims, ((), ())), preferred_element_type=F32)  31.3 us
    all_to_all x1, blocking collectives, shards(): lax.all_to_all(back, 'ts', split_axis=0, concat_axis=1, tiled=True, axis_...  10.8 us
  transfers between devices with their start and end apart: 5, of which 4 were waited for; matrix products, arithmetic and copies ran while one was open for 8% of the time, Pallas kernels for 0%

profile of v1, /device:TPU:8, one launch (start us, length us, event | category | flops | bytes accessed | tf_op | source)
XLA Modules:
  0.0 319.5 jit_solution(12852479243256317759)
XLA Ops:
  7.2 2.2 collective-permute-start
  9.4 2.5 constant_dynamic-update-slice_fusion.3
  11.9 2.5 constant_dynamic-update-slice_fusion.2
  14.4 1.0 dynamic-slice_convert_fusion
  15.4 0.8 dynamic_slice.10
  16.3 0.8 dynamic_slice.11
  17.0 1.2 convolution_convert_fusion.1
  18.2 1.1 convolution_convert_fusion.3
  19.3 0.7 pad_maximum_fusion.2
  20.2 3.5 %fusion.148 = f32[256,256]{1,0:T(8,128)S(1)} fusion(bf16[256,5120]{1,0:T(8,128)(2,1)} %constant_dynamic-update-slice_fusion.2), kind=kOutput, calls=%fused_computation.247 | convolution fusion | flops 671088640 | bytes 2883584 | tf_op jit(solution)/shard_map/dot_general | solution.py:14
  23.7 1.0 convolution_convert_fusion.4
  24.8 0.2 pad_slice_fusion
  25.1 0.8 copy-done.8
  26.1 0.2 fusion.76
  26.2 0.2 convolution_add_fusion.27
  26.6 0.2 convolution_add_fusion.25
  26.7 0.2 convolution_add_fusion.24
  27.5 0.2 convolution_add_fusion.19
  27.8 0.2 convolution_add_fusion.17
  28.0 0.2 convolution_add_fusion.16
  28.8 0.2 convolution_add_fusion.11
  29.1 0.2 convolution_add_fusion.9
  29.3 0.2 convolution_add_fusion.8
  29.9 0.2 convolution_add_fusion.4
  30.1 0.2 fusion.43
  30.5 0.3 fusion.17
  30.8 14.8 %all-reduce.5.cloned.1.call-done = bf16[384,384]{1,0:T(8,128)(2,1)} async-done(((bf16[384,384]{1,0:T(8,128)(2,1)}), bf16[384,384]{1,0:T(8,128)(2,1)}) %all-reduce.5.cloned.1.call-update) | async-done | bytes 294928 | tf_op jit(solution)/shard_map/psum | solution.py:96
  45.6 94.4 %all-reduce.7.cloned.1.call-done = bf16[384,384]{1,0:T(8,128)(2,1)} async-done(((bf16[384,384]{1,0:T(8,128)(2,1)}), bf16[384,384]{1,0:T(8,128)(2,1)}) %all-reduce.7.cloned.1.call-update) | async-done | bytes 294928 | tf_op jit(solution)/shard_map/psum | solution.py:96
  140.1 1.1 fusion.7
  141.2 0.2 fusion.146
  141.6 0.7 copy-done.1
  142.3 0.3 convolution_convert_fusion.8
  142.6 0.2 fusion.71
  142.8 0.9 multiply_reduce_fusion.3
  143.7 0.3 fusion.8
  144.0 0.7 copy-done.7
  144.7 1.0 copy.12
  145.8 4.5 %all-to-all-start = ((bf16[2,160,512]{2,0,1:T(2,128)(2,1)}), bf16[2,160,512]{2,0,1:T(2,128)(2,1)}, u32[]{:S(2)}, u32[]{:S(2)}) async-start(bf16[2,160,512]{2,0,1:T(2,128)(2,1)} %copy.12), calls=%async_computation | async-start | bytes 655360 | tf_op jit(solution)/shard_map/all_to_all | solution.py:118
  150.3 6.3 %all-to-all-done = bf16[2,160,512]{2,0,1:T(2,128)(2,1)} async-done(((bf16[2,160,512]{2,0,1:T(2,128)(2,1)}), bf16[2,160,512]{2,0,1:T(2,128)(2,1)}, u32[]{:S(2)}, u32[]{:S(2)}) %all-to-all-start) | async-done | bytes 327712 | tf_op jit(solution)/shard_map/all_to_all | solution.py:118
  156.6 1.8 copy.13
  158.3 1.8 reshape.248
  160.1 1.2 fusion.147
  161.5 1.2 convolution_convert_fusion.7
  162.7 0.3 multiply_reduce_fusion.2
  163.1 0.3 fusion.12
  163.3 0.2 fusion.13
  163.6 0.2 convolution_convert_fusion.6
  163.8 0.8 pad_maximum_fusion.1
  164.6 1.8 reshape.249
  166.3 10.8 %all_to_all.30 = bf16[16,20,512]{2,1,0:T(8,128)(2,1)S(1)} all-to-all(bf16[16,20,512]{2,1,0:T(8,128)(2,1)} %reshape.249), channel_id=1, replica_groups={{0,1,2,3,4,5,6,7},{8,9,10,11,12,13,14,15},{16,17,18,19,20,21,22,23},{24..., dimensions={0} | all-to-all | bytes 655360 | tf_op jit(solution)/shard_map/all_to_all | solution.py:127
  177.1 0.3 copy.18
  177.5 0.9 copy.15
  178.4 1.8 reshape.250
  180.2 1.2 multiply_reduce_fusion.1
  181.4 1.3 convolution_multiply_fusion.6
  182.7 2.4 fusion.16
  185.1 0.3 multiply_reduce_fusion
  185.5 0.3 fusion.14
  185.8 0.2 fusion.15
  186.1 0.2 convolution_convert_fusion.5
  186.3 1.0 convolution_convert_fusion.2
  187.3 5.7 %convolution_convert_fusion = bf16[320,5120]{1,0:T(8,128)(2,1)} fusion(bf16[128,5120]{1,0:T(8,128)(2,1)} %param.18, bf16[128,5120]{1,0:T(8,128)(2,1)} %param.17, bf16[128,5120]{1,0:T(8,128)(2,1)} %param.12, bf16[320,128]{1,0:T(8,128)(2,1)S(1)} %slice-done, bf16[320,128]{1,0:T(8,128)(2,1)S(1)} %convolution_convert_fusion.8, bf16[320,128]{1,0:T(8,128)(2,1)S(1)} %fusion.43), kind=kOutput, calls=%fused_computation | convolution fusion | flops 1272463360 | bytes 7454720 | tf_op jit(solution)/shard_map/dot_general | solution.py:14
  193.0 118.1 %all-reduce.9.cloned.1.call-done = bf16[128,384]{1,0:T(8,128)(2,1)} async-done(((bf16[128,384]{1,0:T(8,128)(2,1)}), bf16[128,384]{1,0:T(8,128)(2,1)}) %all-reduce.9.cloned.1.call-update) | async-done | bytes 98320 | tf_op jit(solution)/shard_map/psum | solution.py:143
  311.1 1.9 fusion.129
  (65 shorter events, 3.4 us)
Async XLA Ops:
  7.2 16.5 %copy-start = (bf16[2,4,40,5120]{3,2,1,0:T(8,128)(2,1)S(1)}, bf16[2,4,40,5120]{3,2,1,0:T(8,128)(2,1)}, u32[]{:S(2)}) copy-start(bf16[2,4,40,5120]{3,2,1,0:T(8,128)(2,1)} %param.19) | copy-start | bytes 9830404
  7.2 38.4 %all-reduce.5.cloned.1.call-start = ((), (), s32[]{:S(2)}) async-start(), calls=%async_computation.2 | async-start | bytes 589824 | tf_op jit(solution)/shard_map/psum | solution.py:96
  7.2 17.5 %collective-permute-start = (bf16[2,4,40,128]{3,2,1,0:T(8,128)(2,1)}, bf16[2,4,40,128]{3,2,1,0:T(8,128)(2,1)S(1)}, u32[]{:S(2)}, u32[]{:S(2)}) collective-permute-start(bf16[2,4,40,128]{3,2,1,0:T(8,128)(2,1)} %param.10), channel_id=1, source_target_pairs={{0,1},{1,2},{2,3},{3,4},{4,5},{5,6},{6,7},{7,8},{8,9},{9,10},{10,1... | collective-permute-start | bytes 245768 | tf_op jit(solution)/shard_map/ppermute | solution.py:86
  9.4 7.6 %copy-start.13 = (bf16[160,384]{1,0:T(8,128)(2,1)S(1)}, bf16[160,384]{1,0:T(8,128)(2,1)}, u32[]{:S(2)}) copy-start(bf16[160,384]{1,0:T(8,128)(2,1)} %param.16) | copy-start | bytes 368644
  15.4 2.8 copy-start.6
  20.1 120.0 %all-reduce.7.cloned.1.call-start = ((), (), s32[]{:S(2)}) async-start(), calls=%async_computation.3 | async-start | bytes 589824 | tf_op jit(solution)/shard_map/psum | solution.py:96
  20.1 3.5 %copy-start.5 = (bf16[128,5120]{1,0:T(8,128)(2,1)S(1)}, bf16[128,5120]{1,0:T(8,128)(2,1)}, u32[]{:S(2)}) copy-start(bf16[128,5120]{1,0:T(8,128)(2,1)} %param.18) | copy-start | bytes 3932164
  23.7 6.8 %copy-start.3 = (f32[256,256]{1,0:T(8,128)}, f32[256,256]{1,0:T(8,128)S(1)}, u32[]{:S(2)}) copy-start(f32[256,256]{1,0:T(8,128)S(1)} %fusion.148) | copy-start | bytes 786436
  23.7 1.1 copy-start.12
  24.7 1.2 copy-start.8
  140.1 2.5 copy-start.4
  141.2 1.3 copy-start.10
  141.2 2.5 copy-start.14
  141.5 0.8 copy-start.1
  144.0 0.7 copy-start.7
  145.8 10.8 %all-to-all-start = ((bf16[2,160,512]{2,0,1:T(2,128)(2,1)}), bf16[2,160,512]{2,0,1:T(2,128)(2,1)}, u32[]{:S(2)}, u32[]{:S(2)}) async-start(bf16[2,160,512]{2,0,1:T(2,128)(2,1)} %copy.12), calls=%async_computation | async-start | bytes 655360 | tf_op jit(solution)/shard_map/all_to_all | solution.py:118
  150.3 160.8 %all-reduce.9.cloned.1.call-start = ((), (), s32[]{:S(2)}) async-start(), calls=%async_computation.4 | async-start | bytes 196608 | tf_op jit(solution)/shard_map/psum | solution.py:143
  160.1 2.5 copy-start.9
  182.7 2.4 copy-start.2
  182.7 2.4 copy-start.11
  185.4 1.9 slice-start
Sparse Core Ops, SparseCore 0:
  20.2 25.3 all-reduce.4
  49.0 91.0 all-reduce.6
  187.4 123.6 all-reduce.8
